TPU v7x, 256 devices: a whole 4x4x8 slice. The times are simulated.
256 devices in a mesh: row: 16 (over z, core), col: 8 (over x_hi, y), feat: 2 (over x_lo).
Axes of the slice: x: 4 (x_hi: 2, x_lo: 2; x = x_hi * 2 + x_lo), y: 4, z: 8, core: 2. Of those that a mesh axis runs over, the one named last changes fastest.
Arguments:
- features: bfloat16 [65536, 256], P(('col', 'row'), 'feat'), may hold values from -6 to 6
- tile_rows: int32 [16, 8, 256], P('row', 'col'), may hold values from 0 to 31, as said below
- tile_cols: int32 [16, 8, 256], P('row', 'col'), may hold values from 0 to 63
- tile_count: int32 [16, 8], P('row', 'col'), may hold values from 64 to 256, as said below
- tile_values: bfloat16 [16, 8, 256, 128, 128], P('row', 'col'), may hold values from -0.21875 to 0.21875
- weights: bfloat16 [256, 256], replicated, may hold values from -0.375 to 0.375
- cotangent: bfloat16 [65536, 256], P(('row', 'col'), 'feat'), may hold values from -6 to 6
Outputs:
- activated: bfloat16 [65536, 256], P(('row', 'col'), 'feat')
- feature_grad: bfloat16 [65536, 256], P(('col', 'row'), 'feat')
- weight_grad: float32 [256, 256], P('feat')
Inputs may be any that keep to these rules, and one draw needn't show every extreme that they name: `tile_rows`: block rows of a cell, unevenly loaded. `tile_count`: some cell has all 256 slots live.
All inputs are finite; a program needn't handle non-finite values.
Results may differ from a plain program's by a relative error of at most 0.027.
Values may be sent and summed in bfloat16 or wider, within the bound.
A program may use at most 128 MiB of HBM per device.

v0:
```python
import jax
import jax.numpy as jnp
from jax import lax
from jax.sharding import PartitionSpec as P


def shards(features, tile_rows, tile_cols, tile_count, tile_values, weights, cotangent):
    width = tile_values.shape[-1]
    slots = tile_values.shape[2]
    local_tiles = tile_values[0, 0]
    block_rows = tile_rows[0, 0]
    block_cols = tile_cols[0, 0]
    live_mask = (jnp.arange(slots) < tile_count[0, 0]).astype(jnp.float32)
    n_rowdev = lax.axis_size("row")
    n_coldev = lax.axis_size("col")
    local_blocks = features.shape[0] // width
    feat_half = features.shape[1]
    feat_index = lax.axis_index("feat")
    row_blocks = local_blocks * n_coldev
    col_blocks = local_blocks * n_rowdev
    node_total = features.shape[0] * n_rowdev * n_coldev
    panel = lax.all_gather(features, "row", axis=0, tiled=True)
    gathered = panel.reshape(col_blocks, width, feat_half)[block_cols]
    products = jnp.einsum("tij,tjf->tif", local_tiles, gathered, preferred_element_type=jnp.float32)
    products = products * live_mask[:, None, None]
    partial_value = (
        jnp.zeros((row_blocks, width, feat_half), jnp.float32).at[block_rows].add(products)
    )
    summed = lax.psum_scatter(
        partial_value.reshape(row_blocks * width, feat_half).astype(jnp.bfloat16),
        "col",
        scatter_dimension=0,
        tiled=True,
    )
    weight_rows = lax.dynamic_slice_in_dim(weights, feat_index * feat_half, feat_half, 0)
    mix_term = jnp.dot(summed, weight_rows, preferred_element_type=jnp.float32)
    hidden = lax.psum_scatter(
        mix_term.astype(jnp.bfloat16), "feat", scatter_dimension=1, tiled=True
    ).astype(jnp.float32)
    negative = jnp.minimum(hidden, 0.0)
    activated = jnp.where(hidden > 0, hidden, jnp.expm1(negative)).astype(jnp.bfloat16)
    slope_factor = jnp.where(hidden > 0, 1.0, jnp.exp(negative))
    grad_out = (cotangent.astype(jnp.float32) * slope_factor).astype(jnp.bfloat16)
    grad_whole = lax.all_gather(grad_out, "feat", axis=1, tiled=True)
    weight_term = lax.dot_general(
        summed, grad_whole, (((0,), (0,)), ((), ())), preferred_element_type=jnp.float32
    )
    n_feat = lax.axis_size("feat")
    slots = jnp.zeros((n_feat,) + weight_term.shape, jnp.float32)
    slots = lax.dynamic_update_slice_in_dim(slots, weight_term[None], feat_index, 0)
    slots = lax.psum(slots, ("row", "col", "feat"))
    weight_grad = lax.dynamic_index_in_dim(slots, feat_index, 0, keepdims=False) * node_total ** (
        -0.5
    )
    spread = lax.dot_general(
        grad_whole, weight_rows, (((1,), (1,)), ((), ())), preferred_element_type=jnp.float32
    ).astype(jnp.bfloat16)
    spread_panel = lax.all_gather(spread, "col", axis=0, tiled=True)
    spread_blocks = spread_panel.reshape(row_blocks, width, feat_half)[block_rows]
    back_products = jnp.einsum(
        "tji,tjf->tif", local_tiles, spread_blocks, preferred_element_type=jnp.float32
    )
    back_products = back_products * live_mask[:, None, None]
    back_partial = (
        jnp.zeros((col_blocks, width, feat_half), jnp.float32).at[block_cols].add(back_products)
    )
    back_summed = lax.psum_scatter(
        back_partial.reshape(col_blocks * width, feat_half).astype(jnp.bfloat16),
        "row",
        scatter_dimension=0,
        tiled=True,
    )
    return (activated, back_summed, weight_grad)


def solution(mesh):
    return jax.shard_map(
        shards,
        mesh=mesh,
        in_specs=(
            P(("col", "row"), "feat"),
            P("row", "col", None),
            P("row", "col", None),
            P("row", "col"),
            P("row", "col", None, None, None),
            P(),
            P(("row", "col"), "feat"),
        ),
        out_specs=(P(("row", "col"), "feat"), P(("col", "row"), "feat"), P("feat", None)),
        check_vma=False,
    )
```

profile of v0, /device:TPU:2, one launch (start us, length us, event | category | flops | bytes accessed | tf_op | source)
XLA Modules:
  0.0 605.1 jit_solution(15216501221385841070)
XLA Ops:
  7.2 0.0 copy-start
  7.2 0.0 all-gather.3.cloned.1.call-start
  7.2 0.7 all-gather.3.cloned.1.call-update
  7.9 0.0 reduce-scatter.6.cloned.1.call-start
  8.6 0.7 compare_select_fusion
  9.3 43.2 %all-gather.3.cloned.1.call-done = bf16[8192,128]{1,0:T(8,128)(2,1)} async-done(((bf16[512,128]{1,0:T(8,128)(2,1)}), bf16[8192,128]{1,0:T(8,128)(2,1)}) %all-gather.3.cloned.1.call-update) | async-done | bytes 2097168 | tf_op jit(solution)/shard_map/all_gather | solution.py:22
  52.6 10.2 %gather_fusion = bf16[256,128,128]{2,1,0:T(8,128)(2,1)} fusion(bf16[64,128,128]{2,1,0:T(8,128)(2,1)} %bitcast.36, s32[1024]{0:T(1024)S(1)} %pad_clamp_fusion.1), kind=kCustom, calls=%fused_computation | custom fusion | bytes 16778240 | tf_op jit(solution)/shard_map/gather | solution.py:23
  62.8 13.0 %multiply_bitcast_fusion.1 = f32[256,128,128]{1,2,0:T(8,128)} fusion(bf16[256,128,128]{2,1,0:T(8,128)(2,1)} %gather_fusion, bf16[1,1,256,128,128]{4,3,2,1,0:T(8,128)(2,1)} %param.11, f32[256]{0:T(256)S(1)} %compare_convert_fusion), kind=kOutput, calls=%fused_computation.5 | convolution fusion | flops 1077936128 | bytes 33555456 | tf_op jit(solution)/shard_map/tij,tjf->tif/dot_general | solution.py:24
  75.8 17.4 %copy.17 = f32[256,128,128]{2,1,0:T(8,128)} copy(f32[256,128,128]{1,2,0:T(8,128)} %multiply_bitcast_fusion.1) | data formatting | bytes 33554432 | tf_op jit(solution)/shard_map/mul | solution.py:25
  93.2 0.2 broadcast_in_dim.22
  93.5 0.0 copy-start.3
  93.5 33.2 %scatter_fusion = f32[32,128,128]{2,1,0:T(8,128)S(1)} fusion(f32[32,128,128]{2,1,0:T(8,128)S(1)} %broadcast_in_dim.22, s32[256]{0:T(256)S(1)} %bitcast.43, f32[256,128,128]{2,1,0:T(8,128)} %copy.17), kind=kCustom, calls=%fused_computation.2 | custom fusion | flops 4194304 | bytes 50332672 | tf_op jit(solution)/shard_map/scatter-add | solution.py:27
  126.7 1.1 convert_element_type.38
  127.8 0.0 reduce-scatter.6.cloned.1.call-update
  127.8 0.0 reduce-scatter.10.cloned.1.call-start
  127.9 74.5 %reduce-scatter.6.cloned.1.call-done = bf16[512,128]{1,0:T(8,128)(2,1)} async-done(((bf16[4096,128]{1,0:T(8,128)(2,1)}), bf16[512,128]{1,0:T(8,128)(2,1)}) %reduce-scatter.6.cloned.1.call-update) | async-done | bytes 131088 | tf_op jit(solution)/shard_map/reduce_scatter | solution.py:29
  202.3 0.0 copy-done
  202.4 1.1 convolution_convert_fusion
  203.5 0.8 copy.22
  204.3 0.0 reduce-scatter.10.cloned.1.call-update
  204.3 0.0 all-gather.5.cloned.1.call-start
  204.4 16.0 %reduce-scatter.10.cloned.1.call-done = bf16[128,512]{1,0:T(8,128)(2,1)} async-done(((bf16[256,512]{1,0:T(8,128)(2,1)}), bf16[128,512]{1,0:T(8,128)(2,1)}) %reduce-scatter.10.cloned.1.call-update) | async-done | bytes 131088
  220.4 1.0 copy.23
  221.4 0.0 copy-done.3
  221.5 0.8 fusion.7
  222.3 5.9 all_gather.10
  228.2 0.9 convolution_convert_fusion.1
  229.0 0.0 all-gather.5.cloned.1.call-update
  229.1 0.0 all-reduce.2.cloned.1.call-start
  229.2 1.1 fusion.2
  230.3 0.0 copy-start.2
  230.3 0.7 copy-done.2
  231.0 0.0 all-reduce.2.cloned.1.call-update
  231.0 0.2 reduce-scatter.8.cloned.1.call-start
  231.3 50.6 %all-gather.5.cloned.1.call-done = bf16[4096,128]{1,0:T(8,128)(2,1)} async-done(((bf16[512,128]{1,0:T(8,128)(2,1)}), bf16[4096,128]{1,0:T(8,128)(2,1)}) %all-gather.5.cloned.1.call-update) | async-done | bytes 1048592 | tf_op jit(solution)/shard_map/all_gather | solution.py:58
  281.9 9.8 %gather_fusion.1 = bf16[256,128,128]{2,1,0:T(8,128)(2,1)} fusion(bf16[32,128,128]{2,1,0:T(8,128)(2,1)} %bitcast.35, s32[1024]{0:T(1024)S(1)} %pad_clamp_fusion), kind=kCustom, calls=%fused_computation.1 | custom fusion | bytes 16778240 | tf_op jit(solution)/shard_map/gather | solution.py:59
  291.7 15.4 %multiply_bitcast_fusion = f32[256,128,128]{1,2,0:T(8,128)} fusion(bf16[256,128,128]{2,1,0:T(8,128)(2,1)} %gather_fusion.1, bf16[1,1,256,128,128]{4,3,2,1,0:T(8,128)(2,1)} %param.11, f32[256]{0:T(256)S(1)} %compare_convert_fusion), kind=kOutput, calls=%fused_computation.4 | convolution fusion | flops 1077936128 | bytes 33555456 | tf_op jit(solution)/shard_map/tji,tjf->tif/dot_general | solution.py:60
  307.1 17.5 %copy.19 = f32[256,128,128]{2,1,0:T(8,128)} copy(f32[256,128,128]{1,2,0:T(8,128)} %multiply_bitcast_fusion) | data formatting | bytes 33554432 | tf_op jit(solution)/shard_map/mul | solution.py:63
  324.6 2.5 broadcast_in_dim.23
  327.0 0.0 copy-start.1
  327.0 52.1 %scatter_fusion.1 = f32[64,128,128]{2,1,0:T(8,128)} fusion(f32[64,128,128]{2,1,0:T(8,128)} %broadcast_in_dim.23, s32[256]{0:T(256)S(1)} %bitcast.42, f32[256,128,128]{2,1,0:T(8,128)} %copy.19), kind=kCustom, calls=%fused_computation.3 | custom fusion | flops 4194304 | bytes 50332672 | tf_op jit(solution)/shard_map/scatter-add | solution.py:65
  379.1 3.9 convert_element_type.46
  383.0 0.0 reduce-scatter.8.cloned.1.call-update
  383.1 154.2 %all-reduce.2.cloned.1.call-done = f32[2,128,256]{2,1,0:T(8,128)} async-done(((f32[2,128,256]{2,1,0:T(8,128)}), f32[2,128,256]{2,1,0:T(8,128)}) %all-reduce.2.cloned.1.call-update) | async-done | bytes 262160 | tf_op jit(solution)/shard_map/psum | solution.py:51
  537.3 1.6 multiply_bitcast_fusion.2
  538.8 59.4 %reduce-scatter.8.cloned.1.call-done = bf16[512,128]{1,0:T(8,128)(2,1)} async-done(((bf16[8192,128]{1,0:T(8,128)(2,1)}), bf16[512,128]{1,0:T(8,128)(2,1)}) %reduce-scatter.8.cloned.1.call-update) | async-done | bytes 131088 | tf_op jit(solution)/shard_map/reduce_scatter | solution.py:67
  598.3 0.0 copy-done.1
  (4 shorter events, 0.0 us)
Async XLA Ops:
  7.2 195.2 %copy-start = (bf16[256,256]{1,0:T(8,128)(2,1)S(1)}, bf16[256,256]{1,0:T(8,128)(2,1)}, u32[]{:S(2)}) copy-start(bf16[256,256]{1,0:T(8,128)(2,1)} %param.12) | copy-start | bytes 393220
  7.2 45.4 %all-gather.3.cloned.1.call-start = ((), (), s32[]{:S(2)}) async-start(), calls=%async_computation.3 | async-start | bytes 2228224 | tf_op jit(solution)/shard_map/all_gather | solution.py:22
  7.9 194.4 %reduce-scatter.6.cloned.1.call-start = ((), (), s32[]{:S(2)}) async-start(), calls=%async_computation.4 | async-start | bytes 1179648 | tf_op jit(solution)/shard_map/reduce_scatter | solution.py:29
  93.5 128.0 %copy-start.3 = (bf16[512,128]{1,0:T(8,128)(2,1)S(1)}, bf16[512,128]{1,0:T(8,128)(2,1)}, u32[]{:S(2)}) copy-start(bf16[512,128]{1,0:T(8,128)(2,1)} %param.13) | copy-start | bytes 393220
  127.8 92.6 %reduce-scatter.10.cloned.1.call-start = ((), (), s32[]{:S(2)}) async-start(), calls=%async_computation.8 | async-start | bytes 393216
  204.3 77.5 %all-gather.5.cloned.1.call-start = ((), (), s32[]{:S(2)}) async-start(), calls=%async_computation.5 | async-start | bytes 1179648 | tf_op jit(solution)/shard_map/all_gather | solution.py:58
  229.1 308.2 %all-reduce.2.cloned.1.call-start = ((), (), s32[]{:S(2)}) async-start(), calls=%async_computation.7 | async-start | bytes 524288 | tf_op jit(solution)/shard_map/psum | solution.py:51
  230.3 0.7 copy-start.2
  231.0 367.2 %reduce-scatter.8.cloned.1.call-start = ((), (), s32[]{:S(2)}) async-start(), calls=%async_computation.6 | async-start | bytes 2228224 | tf_op jit(solution)/shard_map/reduce_scatter | solution.py:67
  327.0 271.2 %copy-start.1 = (bf16[256,256]{1,0:T(8,128)(2,1)S(1)}, bf16[256,256]{1,0:T(8,128)(2,1)}, u32[]{:S(2)}) copy-start(bf16[256,256]{1,0:T(8,128)(2,1)} %param.12) | copy-start | bytes 393220
Sparse Core Ops, SparseCore 0:
  9.8 42.6 all-gather.2
  127.9 74.3 reduce-scatter.5
  205.0 15.3 reduce-scatter.9
  229.2 52.6 all-gather.4
  287.2 250.0 all-reduce.1
  540.2 57.9 reduce-scatter.7
where the time goes:
time: 607 us; the launch traced here: 605 us
  waiting for transfers between devices  399 us (66%)
  other arithmetic  93.4 us (15%)
  local copies, waits for them, and re-layouts  60.2 us (10%)
  matrix products  31.5 us (5%)
  between operations  14.9 us (2%)
    psum x1, waiting for transfers between devices, shards(): slots = lax.psum(slots, ('row', 'col', 'feat'))  154 us
    reduce_scatter x1, waiting for transfers between devices, shards(): lax.psum_scatter(partial_value.reshape(row_blocks * width, feat_half).ast...  74.5 us
    reduce_scatter x1, waiting for transfers between devices, shards(): lax.psum_scatter(back_partial.reshape(col_blocks * width, feat_half).asty...  59.4 us
    scatter-add x1, other arithmetic, shards(): jnp.zeros((col_blocks, width, feat_half), jnp.float32).at[block_cols]  52.1 us
    all_gather x1, waiting for transfers between devices, shards(): spread_panel = lax.all_gather(spread, 'col', axis=0, tiled=True)  50.6 us
    all_gather x1, waiting for transfers between devices, shards(): panel = lax.all_gather(features, 'row', axis=0, tiled=True)  43.2 us
    scatter-add x1, other arithmetic, shards(): jnp.zeros((row_blocks, width, feat_half), jnp.float32).at[block_rows]  33.2 us
    mul x1, local copies, waits for them, and re-layouts, shards(): back_products = back_products * live_mask[:, None, None]  17.5 us
  transfers between devices with their start and end apart: 6, of which 6 were waited for; matrix products, arithmetic and copies ran while one was open for 17% of the time, Pallas kernels for 0%

commit v1 on v0

--- a/solution.py
+++ b/solution.py
@@ -2,6 +2,7 @@
 import jax.numpy as jnp
 from jax import lax
 from jax.sharding import PartitionSpec as P
+from jax.lax import axis_index, axis_size, ppermute
 
 
 def shards(features, tile_rows, tile_cols, tile_count, tile_values, weights, cotangent):
@@ -19,7 +20,27 @@
     row_blocks = local_blocks * n_coldev
     col_blocks = local_blocks * n_rowdev
     node_total = features.shape[0] * n_rowdev * n_coldev
-    panel = lax.all_gather(features, "row", axis=0, tiled=True)
+
+    def islands_handle(vector, row_axis):
+        axis_total = axis_size(row_axis)
+        column = []
+        for dd in range(axis_total):
+            column.append((dd, (dd + 1) % axis_total))
+        steps_seen = []
+        for dd in range(axis_total):
+            steps_seen.append((dd, (dd - 1) % axis_total))
+        mid_arr, v_now = ([vector], [vector])
+        for _ in range(axis_total // 2):
+            mid_arr.append(ppermute(mid_arr[-1], axis_name=row_axis, perm=column))
+        for _ in range((axis_total - 1) // 2):
+            v_now.append(ppermute(v_now[-1], axis_name=row_axis, perm=steps_seen))
+        raw_out = jnp.concatenate([*mid_arr[::-1], *v_now[1:]], axis=0)
+        taken_in = jnp.roll(
+            raw_out, (axis_index(row_axis) - axis_total // 2) * vector.shape[0], axis=0
+        )
+        return taken_in
+
+    panel = islands_handle(features, "row")
     gathered = panel.reshape(col_blocks, width, feat_half)[block_cols]
     products = jnp.einsum("tij,tjf->tif", local_tiles, gathered, preferred_element_type=jnp.float32)
     products = products * live_mask[:, None, None]

time: 607 us -> 611 us (level)
  starting transfers between devices: 0.42 us -> 21.5 us
  waiting for transfers between devices: 399 us -> 382 us
    all_gather x1 -> x0, waiting for transfers between devices: 43.2 us -> none  [shards(): panel = lax.all_gather(features, 'row', axis=0, tiled=True)]
    ppermute x0 -> x15, waiting for transfers between devices: none -> 24.9 us  [the longest x8 24 us: islands_handle(): mid_arr.append(ppermute(mid_arr[-1], axis_name=row_axis, perm=column))]
    ppermute x0 -> x15, starting transfers between devices: none -> 21.1 us  [the longest x7 21.1 us: islands_handle(): v_now.append(ppermute(v_now[-1], axis_name=row_axis, perm=steps_seen))]
    unnamed x7 -> x6, waiting for transfers between devices: 16.8 us -> 16.1 us
  transfers between devices with their start and end apart: 6 -> 20, of which waited for: 6 -> 17; matrix products, arithmetic and copies ran while one was open for 17% -> 17% of each run, Pallas kernels for 0% -> 0%
where the time goes in v1:
time: 611 us; the launch traced here: 610 us
  waiting for transfers between devices  382 us (63%)
  other arithmetic  93.1 us (15%)
  local copies, waits for them, and re-layouts  60.3 us (10%)
  matrix products  31.6 us (5%)
  starting transfers between devices  21.5 us (4%)
  between operations  14.8 us (2%)
    psum x1, waiting for transfers between devices, shards(): slots = lax.psum(slots, ('row', 'col', 'feat'))  154 us
    reduce_scatter x1, waiting for transfers between devices, shards(): lax.psum_scatter(partial_value.reshape(row_blocks * width, feat_half).ast...  76.7 us
    reduce_scatter x1, waiting for transfers between devices, shards(): lax.psum_scatter(back_partial.reshape(col_blocks * width, feat_half).asty...  59.4 us
    scatter-add x1, other arithmetic, shards(): jnp.zeros((col_blocks, width, feat_half), jnp.float32).at[block_cols]  51.8 us
    all_gather x1, waiting for transfers between devices, shards(): spread_panel = lax.all_gather(spread, 'col', axis=0, tiled=True)  50.6 us
    scatter-add x1, other arithmetic, shards(): jnp.zeros((row_blocks, width, feat_half), jnp.float32).at[block_rows]  33.2 us
    ppermute x8, waiting for transfers between devices, islands_handle(): mid_arr.append(ppermute(mid_arr[-1], axis_name=row_axis, perm=column))  24 us
    ppermute x7, starting transfers between devices, islands_handle(): v_now.append(ppermute(v_now[-1], axis_name=row_axis, perm=steps_seen))  21.1 us
  transfers between devices with their start and end apart: 20, of which 17 were waited for; matrix products, arithmetic and copies ran while one was open for 17% of the time, Pallas kernels for 0%

profile of v1, /device:TPU:2, one launch (start us, length us, event | category | flops | bytes accessed | tf_op | source)
XLA Modules:
  0.0 609.5 jit_solution(36887731074195980)
XLA Ops:
  7.3 8.1 %collective-permute-done = bf16[512,128]{1,0:T(8,128)(2,1)S(1)} collective-permute-done((bf16[512,128]{1,0:T(8,128)(2,1)}, bf16[512,128]{1,0:T(8,128)(2,1)S(1)}, u32[]{:S(2)}, u32[]{:S(2)}) %collective-permute-start) | collective-permute-done | bytes 131104 | tf_op jit(solution)/shard_map/ppermute | solution.py:34
  15.4 3.0 collective-permute-start.8
  18.4 2.6 collective-permute-done.1
  21.0 0.2 collective-permute-done.8
  21.2 3.0 collective-permute-start.9
  24.2 2.4 collective-permute-done.2
  26.6 0.1 collective-permute-done.9
  26.7 3.1 collective-permute-start.10
  29.8 2.4 collective-permute-done.3
  32.3 3.1 collective-permute-start.11
  35.4 2.4 collective-permute-done.4
  38.5 3.0 collective-permute-start.12
  41.5 2.0 collective-permute-done.5
  43.4 0.7 compare_select_fusion
  44.1 3.0 collective-permute-start.13
  47.1 1.9 collective-permute-done.6
  49.1 0.6 collective-permute-done.13
  49.6 3.1 collective-permute-start.14
  52.7 1.9 collective-permute-done.7
  54.8 0.9 constant_dynamic-update-slice_fusion.23
  56.4 0.1 constant_dynamic-slice_fusion
  56.6 8.6 %gather_fusion = bf16[256,128,128]{2,1,0:T(8,128)(2,1)} fusion(bf16[64,128,128]{2,1,0:T(8,128)(2,1)S(1)} %bitcast.36, s32[1024]{0:T(1024)S(1)} %pad_clamp_fusion.1), kind=kCustom, calls=%fused_computation | custom fusion | bytes 16778240 | tf_op jit(solution)/shard_map/gather | solution.py:44
  65.2 13.0 %multiply_bitcast_fusion.1 = f32[256,128,128]{1,2,0:T(8,128)} fusion(bf16[256,128,128]{2,1,0:T(8,128)(2,1)} %gather_fusion, bf16[1,1,256,128,128]{4,3,2,1,0:T(8,128)(2,1)} %param.11, f32[256]{0:T(256)S(1)} %compare_convert_fusion), kind=kOutput, calls=%fused_computation.5 | convolution fusion | flops 1077936128 | bytes 33555456 | tf_op jit(solution)/shard_map/tij,tjf->tif/dot_general | solution.py:45
  78.2 17.5 %copy.17 = f32[256,128,128]{2,1,0:T(8,128)} copy(f32[256,128,128]{1,2,0:T(8,128)} %multiply_bitcast_fusion.1) | data formatting | bytes 33554432 | tf_op jit(solution)/shard_map/mul | solution.py:46
  95.7 0.2 broadcast_in_dim.22
  95.9 33.2 %scatter_fusion = f32[32,128,128]{2,1,0:T(8,128)S(1)} fusion(f32[32,128,128]{2,1,0:T(8,128)S(1)} %broadcast_in_dim.22, s32[256]{0:T(256)S(1)} %bitcast.43, f32[256,128,128]{2,1,0:T(8,128)} %copy.17), kind=kCustom, calls=%fused_computation.2 | custom fusion | flops 4194304 | bytes 50332672 | tf_op jit(solution)/shard_map/scatter-add | solution.py:48
  129.1 1.1 convert_element_type.38
  130.4 76.7 %reduce-scatter.6.cloned.1.call-done = bf16[512,128]{1,0:T(8,128)(2,1)} async-done(((bf16[4096,128]{1,0:T(8,128)(2,1)}), bf16[512,128]{1,0:T(8,128)(2,1)}) %reduce-scatter.6.cloned.1.call-update) | async-done | bytes 131088 | tf_op jit(solution)/shard_map/reduce_scatter | solution.py:50
  207.1 1.1 convolution_convert_fusion
  208.2 0.8 copy.22
  209.1 16.0 %reduce-scatter.10.cloned.1.call-done = bf16[128,512]{1,0:T(8,128)(2,1)} async-done(((bf16[256,512]{1,0:T(8,128)(2,1)}), bf16[128,512]{1,0:T(8,128)(2,1)}) %reduce-scatter.10.cloned.1.call-update) | async-done | bytes 131088
  225.1 1.0 copy.23
  226.2 0.8 fusion.7
  227.0 5.9 all_gather.6
  232.9 0.9 convolution_convert_fusion.1
  233.9 1.1 fusion.2
  235.1 0.7 copy-done.2
  235.8 0.2 reduce-scatter.8.cloned.1.call-start
  236.0 50.6 %all-gather.2.cloned.1.call-done = bf16[4096,128]{1,0:T(8,128)(2,1)} async-done(((bf16[512,128]{1,0:T(8,128)(2,1)}), bf16[4096,128]{1,0:T(8,128)(2,1)}) %all-gather.2.cloned.1.call-update) | async-done | bytes 1048592 | tf_op jit(solution)/shard_map/all_gather | solution.py:79
  286.6 9.8 %gather_fusion.1 = bf16[256,128,128]{2,1,0:T(8,128)(2,1)} fusion(bf16[32,128,128]{2,1,0:T(8,128)(2,1)} %bitcast.35, s32[1024]{0:T(1024)S(1)} %pad_clamp_fusion), kind=kCustom, calls=%fused_computation.1 | custom fusion | bytes 16778240 | tf_op jit(solution)/shard_map/gather | solution.py:80
  296.4 15.4 %multiply_bitcast_fusion = f32[256,128,128]{1,2,0:T(8,128)} fusion(bf16[256,128,128]{2,1,0:T(8,128)(2,1)} %gather_fusion.1, bf16[1,1,256,128,128]{4,3,2,1,0:T(8,128)(2,1)} %param.11, f32[256]{0:T(256)S(1)} %compare_convert_fusion), kind=kOutput, calls=%fused_computation.4 | convolution fusion | flops 1077936128 | bytes 33555456 | tf_op jit(solution)/shard_map/tji,tjf->tif/dot_general | solution.py:81
  311.8 17.5 %copy.19 = f32[256,128,128]{2,1,0:T(8,128)} copy(f32[256,128,128]{1,2,0:T(8,128)} %multiply_bitcast_fusion) | data formatting | bytes 33554432 | tf_op jit(solution)/shard_map/mul | solution.py:84
  329.3 2.5 broadcast_in_dim.23
  331.8 51.8 %scatter_fusion.1 = f32[64,128,128]{2,1,0:T(8,128)} fusion(f32[64,128,128]{2,1,0:T(8,128)} %broadcast_in_dim.23, s32[256]{0:T(256)S(1)} %bitcast.42, f32[256,128,128]{2,1,0:T(8,128)} %copy.19), kind=kCustom, calls=%fused_computation.3 | custom fusion | flops 4194304 | bytes 50332672 | tf_op jit(solution)/shard_map/scatter-add | solution.py:86
  383.6 3.9 convert_element_type.46
  387.5 154.5 %all-reduce.2.cloned.1.call-done = f32[2,128,256]{2,1,0:T(8,128)} async-done(((f32[2,128,256]{2,1,0:T(8,128)}), f32[2,128,256]{2,1,0:T(8,128)}) %all-reduce.2.cloned.1.call-update) | async-done | bytes 262160 | tf_op jit(solution)/shard_map/psum | solution.py:72
  542.0 1.6 multiply_bitcast_fusion.2
  543.6 59.4 %reduce-scatter.8.cloned.1.call-done = bf16[512,128]{1,0:T(8,128)(2,1)} async-done(((bf16[8192,128]{1,0:T(8,128)(2,1)}), bf16[512,128]{1,0:T(8,128)(2,1)}) %reduce-scatter.8.cloned.1.call-update) | async-done | bytes 131088 | tf_op jit(solution)/shard_map/reduce_scatter | solution.py:88
  (65 shorter events, 1.0 us)
Async XLA Ops:
  7.2 199.9 %copy-start = (bf16[256,256]{1,0:T(8,128)(2,1)S(1)}, bf16[256,256]{1,0:T(8,128)(2,1)}, u32[]{:S(2)}) copy-start(bf16[256,256]{1,0:T(8,128)(2,1)} %param.12) | copy-start | bytes 393220
  7.2 49.0 %copy-start.3 = (bf16[512,128]{1,0:T(8,128)(2,1)S(1)}, bf16[512,128]{1,0:T(8,128)(2,1)}, u32[]{:S(2)}) copy-start(bf16[512,128]{1,0:T(8,128)(2,1)} %param.7) | copy-start | bytes 393220
  7.2 199.9 %reduce-scatter.6.cloned.1.call-start = ((), (), s32[]{:S(2)}) async-start(), calls=%async_computation.3 | async-start | bytes 1179648 | tf_op jit(solution)/shard_map/reduce_scatter | solution.py:50
  7.2 8.2 %collective-permute-start = (bf16[512,128]{1,0:T(8,128)(2,1)}, bf16[512,128]{1,0:T(8,128)(2,1)S(1)}, u32[]{:S(2)}, u32[]{:S(2)}) collective-permute-start(bf16[512,128]{1,0:T(8,128)(2,1)} %param.7), channel_id=1, source_target_pairs={{0,16},{16,32},{32,48},{48,64},{64,80},{80,96},{96,112},{112,128},... | collective-permute-start | bytes 393224 | tf_op jit(solution)/shard_map/ppermute | solution.py:34
  15.4 5.6 collective-permute-start.1
  15.4 5.8 collective-permute-start.8
  21.0 5.6 collective-permute-start.2
  21.2 5.5 collective-permute-start.9
  26.6 5.6 collective-permute-start.3
  26.7 5.6 collective-permute-start.10
  32.2 5.6 collective-permute-start.4
  32.3 6.2 %collective-permute-start.11 = (bf16[512,128]{1,0:T(8,128)(2,1)S(1)}, bf16[512,128]{1,0:T(8,128)(2,1)S(1)}, u32[]{:S(2)}, u32[]{:S(2)}) collective-permute-start(bf16[512,128]{1,0:T(8,128)(2,1)S(1)} %collective-permute-done.10), channel_id=1, source_target_pairs={{0,240},{16,0},{32,16},{48,32},{64,48},{80,64},{96,80},{112,96},{1... | collective-permute-start | bytes 393224 | tf_op jit(solution)/shard_map/ppermute | solution.py:36
  37.8 5.6 collective-permute-start.5
  38.5 5.6 collective-permute-start.12
  43.4 5.6 collective-permute-start.6
  44.1 5.5 collective-permute-start.13
  49.0 5.6 collective-permute-start.7
  49.6 6.3 %collective-permute-start.14 = (bf16[512,128]{1,0:T(8,128)(2,1)S(1)}, bf16[512,128]{1,0:T(8,128)(2,1)S(1)}, u32[]{:S(2)}, u32[]{:S(2)}) collective-permute-start(bf16[512,128]{1,0:T(8,128)(2,1)S(1)} %collective-permute-done.13), channel_id=1, source_target_pairs={{0,240},{16,0},{32,16},{48,32},{64,48},{80,64},{96,80},{112,96},{1... | collective-permute-start | bytes 393224 | tf_op jit(solution)/shard_map/ppermute | solution.py:36
  129.1 97.0 %copy-start.4 = (bf16[512,128]{1,0:T(8,128)(2,1)S(1)}, bf16[512,128]{1,0:T(8,128)(2,1)}, u32[]{:S(2)}) copy-start(bf16[512,128]{1,0:T(8,128)(2,1)} %param.13) | copy-start | bytes 393220
  130.3 94.8 %reduce-scatter.10.cloned.1.call-start = ((), (), s32[]{:S(2)}) async-start(), calls=%async_computation.7 | async-start | bytes 393216
  209.1 77.5 %all-gather.2.cloned.1.call-start = ((), (), s32[]{:S(2)}) async-start(), calls=%async_computation.4 | async-start | bytes 1179648 | tf_op jit(solution)/shard_map/all_gather | solution.py:79
  233.8 308.2 %all-reduce.2.cloned.1.call-start = ((), (), s32[]{:S(2)}) async-start(), calls=%async_computation.6 | async-start | bytes 524288 | tf_op jit(solution)/shard_map/psum | solution.py:72
  235.0 0.7 copy-start.2
  235.8 367.2 %reduce-scatter.8.cloned.1.call-start = ((), (), s32[]{:S(2)}) async-start(), calls=%async_computation.5 | async-start | bytes 2228224 | tf_op jit(solution)/shard_map/reduce_scatter | solution.py:88
  331.8 271.2 %copy-start.1 = (bf16[256,256]{1,0:T(8,128)(2,1)S(1)}, bf16[256,256]{1,0:T(8,128)(2,1)}, u32[]{:S(2)}) copy-start(bf16[256,256]{1,0:T(8,128)(2,1)} %param.12) | copy-start | bytes 393220
Sparse Core Ops, SparseCore 0:
  130.4 76.6 reduce-scatter.5
  209.7 15.3 reduce-scatter.9
  233.9 52.6 all-gather.1
  291.9 250.0 all-reduce.1
  544.9 57.9 reduce-scatter.7
